TPU v7x, 32 devices: a whole 2x2x4 slice. The times are simulated.
32 devices in a mesh: sec: 8 (over y, x, core), cross: 4 (over z).
Axes of the slice: x: 2, y: 2, z: 4, core: 2. Of those that a mesh axis runs over, the one named last changes fastest.
Arguments:
- rhs_field: float32 [2, 8, 2, 512, 512], P(None, 'sec', None, 'cross'), may hold values from -1.5 to 1.5
- slowness: float32 [8, 512, 512], P('sec', 'cross'), may hold values from 0.25 to 4
- absorb_depth: int32 [8], P('sec'), may hold values from 8 to 64
- line_inverse: bfloat16 [8, 2, 512, 512], P('sec'), may hold values from -1 to 1
- cross_inverse: bfloat16 [8, 2, 512, 512], P('sec', None, 'cross'), may hold values from -1 to 1
Outputs:
- solution: float32 [2, 8, 2, 512, 512], P(None, 'sec', None, 'cross')
- residual: float32 [2, 8, 2, 512, 512], P(None, 'sec', None, 'cross')
All inputs are finite; a program needn't handle non-finite values.
Results may differ from a plain program's by a relative error of at most 0.02.
Values may be sent and summed in bfloat16 or wider, within the bound.
A program may use at most 64 MiB of HBM per device.

v0:
```python
import jax
import jax.numpy as jnp
from jax import lax
from jax.sharding import PartitionSpec as P

SIGMA_TOP = 2.0
CENTER = 128.0 / 30.0
FACE = 14.0 / 30.0
EDGE = 3.0 / 30.0
CORNER = 1.0 / 30.0


def passed_along(shard, axis, by):
    devices = lax.axis_size(axis)
    pairs = [(i, i + by) for i in range(devices) if 0 <= i + by < devices]
    return lax.ppermute(shard, axis, pairs)


def with_halo(cells, sides, width):
    for axis, dim in sides:
        count = lax.axis_size(axis)
        ends = count - 1
        head = lax.slice_in_dim(cells, 0, width, axis=dim)
        tail = lax.slice_in_dim(cells, cells.shape[dim] - width, cells.shape[dim], axis=dim)
        cells = jnp.concatenate(
            [
                lax.ppermute(tail, axis, [(i, (i + 1) % count) for i in range(ends)]),
                cells,
                lax.ppermute(head, axis, [((i + 1) % count, i) for i in range(ends)]),
            ],
            axis=dim,
        )
    return cells


def complex_line(source, matrix):
    real_part = jnp.dot(source[0], matrix[0], preferred_element_type=jnp.float32) - jnp.dot(
        source[1], matrix[1], preferred_element_type=jnp.float32
    )
    imag_part = jnp.dot(source[0], matrix[1], preferred_element_type=jnp.float32) + jnp.dot(
        source[1], matrix[0], preferred_element_type=jnp.float32
    )
    return jnp.stack([real_part, imag_part]).astype(jnp.bfloat16)


def cross_fold(mixed, coupling_rows):
    gathered = lax.all_gather(mixed, "cross", axis=2, tiled=True)
    real_real = jnp.einsum(
        "yk,rkx->ryx", coupling_rows[0], gathered[0], preferred_element_type=jnp.float32
    )
    imag_imag = jnp.einsum(
        "yk,rkx->ryx", coupling_rows[1], gathered[1], preferred_element_type=jnp.float32
    )
    real_imag = jnp.einsum(
        "yk,rkx->ryx", coupling_rows[0], gathered[1], preferred_element_type=jnp.float32
    )
    imag_real = jnp.einsum(
        "yk,rkx->ryx", coupling_rows[1], gathered[0], preferred_element_type=jnp.float32
    )
    real_part = real_real - imag_imag
    imag_part = real_imag + imag_real
    return jnp.stack([real_part, imag_part])


def sweep_section(rhs_local, prior, line_matrix, cross_local):
    item_count = rhs_local.shape[2]
    line_count = rhs_local.shape[3]
    column_count = rhs_local.shape[4]
    source = (rhs_local[:, 0] + prior).astype(jnp.bfloat16)
    mixed = complex_line(source.reshape(2, item_count * line_count, column_count), line_matrix)
    mixed = mixed.reshape(2, item_count, line_count, column_count)
    prior = cross_fold(mixed, cross_local[0])
    outputs = [prior]
    return jnp.stack(outputs, axis=1)


def absorption(absorb_depth, column_count):
    column = jnp.arange(column_count, dtype=jnp.int32)
    distance = jnp.minimum(column, column_count - 1 - column).astype(jnp.float32)
    depth = absorb_depth.astype(jnp.float32)[:, None]
    ramp = jnp.maximum(depth - distance[None, :], 0.0) / depth
    return SIGMA_TOP * ramp * ramp


def operate(field, padded, slowness, absorb_depth):
    layer_count = field.shape[1]
    line_count = field.shape[3]
    column_count = field.shape[4]
    weights = (0.0, FACE, EDGE, CORNER)
    near = jnp.zeros(field.shape, jnp.float32)
    for depth_move in (-1, 0, 1):
        for line_move in (-1, 0, 1):
            for column_move in (-1, 0, 1):
                reach = abs(depth_move) + abs(line_move) + abs(column_move)
                if reach > 0:
                    near = (
                        near
                        + weights[reach]
                        * padded[
                            :,
                            1 + depth_move : 1 + depth_move + layer_count,
                            :,
                            1 + line_move : 1 + line_move + line_count,
                            1 + column_move : 1 + column_move + column_count,
                        ]
                    )
    damping = absorption(absorb_depth, column_count)
    wave_real = slowness[:, None, :, :]
    wave_imag = wave_real * damping[:, None, None, :]
    real_part = CENTER * field[0] - near[0] - (wave_real * field[0] - wave_imag * field[1])
    imag_part = CENTER * field[1] - near[1] - (wave_real * field[1] + wave_imag * field[0])
    return jnp.stack([real_part, imag_part])


def per_device(rhs_field, slowness, absorb_depth, line_inverse, cross_inverse):
    line_matrix = line_inverse[0]
    layer_count = rhs_field.shape[1]
    item_count = rhs_field.shape[2]
    line_count = rhs_field.shape[3]
    column_count = rhs_field.shape[4]
    sections = lax.axis_size("sec")
    start_prior = jnp.zeros((2, item_count, line_count, column_count), jnp.float32)
    first = sweep_section(rhs_field, start_prior, line_matrix, cross_inverse)

    def advance_whole(counter, current):
        prior = passed_along(current[:, layer_count - 1].astype(jnp.bfloat16), "sec", 1).astype(
            jnp.float32
        )
        return sweep_section(rhs_field, prior, line_matrix, cross_inverse)

    solution = lax.fori_loop(0, sections - 1, advance_whole, first)
    padded = with_halo(solution.astype(jnp.bfloat16), (("sec", 1), ("cross", 3)), 1).astype(
        solution.dtype
    )
    padded = jnp.pad(padded, ((0, 0), (0, 0), (0, 0), (0, 0), (1, 1)))
    residual = rhs_field - operate(solution, padded, slowness, absorb_depth)
    return (solution, residual)


def solution(mesh):
    placed = (
        P(None, "sec", None, "cross", None),
        P("sec", "cross", None),
        P("sec"),
        P("sec", None, None, None),
        P("sec", None, "cross", None),
    )
    return jax.shard_map(
        per_device,
        mesh=mesh,
        in_specs=placed,
        out_specs=(P(None, "sec", None, "cross", None), P(None, "sec", None, "cross", None)),
        check_vma=False,
    )
```

profile of v0, /device:TPU:1, one launch (start us, length us, event | category | flops | bytes accessed | tf_op | source)
XLA Modules:
  0.0 556.7 jit_solution(8735741020299506886)
XLA Ops:
  7.2 1.4 convert_element_type.39
  13.2 46.5 %all-gather.3.cloned.1.call-done = bf16[2,2,512,512]{2,3,1,0:T(8,128)(2,1)} async-done(((bf16[2,2,128,512]{2,3,1,0:T(8,128)(2,1)}), bf16[2,2,512,512]{2,3,1,0:T(8,128)(2,1)}) %all-gather.3.cloned.1.call-update) | async-done | bytes 2097168 | tf_op jit(solution)/shard_map/all_gather | solution.py:47
  59.7 1.8 fusion.72
  61.6 1.7 fusion.73
  64.2 452.2 %while.10 = (s32[]{:T(128)}, f32[2,1,2,128,512]{3,4,2,0,1:T(8,128)S(1)}, f32[2,1,2,128,512]{3,4,2,0,1:T(8,128)S(1)}, bf16[2,512,512]{2,1,0:T(8,128)(2,1)S(1)}, bf16[1,2,128,512]{3,2,1,0:T(8,128)(2,1)}, /*index=5*/s32[]{:T(128)}) while((s32[]{:T(128)}, f32[2,1,2,128,512]{3,4,2,0,1:T(8,128)S(1)}, f32[2,1,2,128,512]{3,4,2,0,1:T(8,128)S(1)}, ...), condition=%wide.region_1.0_spmd, body=%wide.region_0.0_spmd.sunk | while | flops 1075838976 | bytes 44040396 | solution.py:131
  65.2 5.2 collective-permute-start
  70.8 6.1 %collective-permute-done = bf16[2,2,128,512]{3,2,1,0:T(8,128)(2,1)} collective-permute-done((bf16[2,2,128,512]{3,2,1,0:T(8,128)(2,1)}, bf16[2,2,128,512]{3,2,1,0:T(8,128)(2,1)}, u32[]{:S(2)}, u32[]{:S(2)}) %collective-permute-start) | collective-permute-done | bytes 524320 | tf_op jit(solution)/shard_map/while/body/eval_jaxpr/ppermute | solution.py:16
  80.6 43.7 %all-gather.5.cloned.1.call-done = bf16[2,2,512,512]{2,3,1,0:T(8,128)(2,1)} async-done(((bf16[2,2,128,512]{2,3,1,0:T(8,128)(2,1)}), bf16[2,2,512,512]{2,3,1,0:T(8,128)(2,1)}) %all-gather.5.cloned.1.call-update) | async-done | bytes 2097168 | tf_op jit(solution)/shard_map/while/body/eval_jaxpr/all_gather | solution.py:47
  124.3 1.8 fusion.150
  126.2 1.7 fusion.148
  129.8 5.2 collective-permute-start
  135.4 6.1 %collective-permute-done = bf16[2,2,128,512]{3,2,1,0:T(8,128)(2,1)} collective-permute-done((bf16[2,2,128,512]{3,2,1,0:T(8,128)(2,1)}, bf16[2,2,128,512]{3,2,1,0:T(8,128)(2,1)}, u32[]{:S(2)}, u32[]{:S(2)}) %collective-permute-start) | collective-permute-done | bytes 524320 | tf_op jit(solution)/shard_map/while/body/eval_jaxpr/ppermute | solution.py:16
  145.2 43.7 %all-gather.5.cloned.1.call-done = bf16[2,2,512,512]{2,3,1,0:T(8,128)(2,1)} async-done(((bf16[2,2,128,512]{2,3,1,0:T(8,128)(2,1)}), bf16[2,2,512,512]{2,3,1,0:T(8,128)(2,1)}) %all-gather.5.cloned.1.call-update) | async-done | bytes 2097168 | tf_op jit(solution)/shard_map/while/body/eval_jaxpr/all_gather | solution.py:47
  188.9 1.8 fusion.150
  190.7 1.7 fusion.148
  194.4 5.2 collective-permute-start
  200.0 6.1 %collective-permute-done = bf16[2,2,128,512]{3,2,1,0:T(8,128)(2,1)} collective-permute-done((bf16[2,2,128,512]{3,2,1,0:T(8,128)(2,1)}, bf16[2,2,128,512]{3,2,1,0:T(8,128)(2,1)}, u32[]{:S(2)}, u32[]{:S(2)}) %collective-permute-start) | collective-permute-done | bytes 524320 | tf_op jit(solution)/shard_map/while/body/eval_jaxpr/ppermute | solution.py:16
  209.8 43.7 %all-gather.5.cloned.1.call-done = bf16[2,2,512,512]{2,3,1,0:T(8,128)(2,1)} async-done(((bf16[2,2,128,512]{2,3,1,0:T(8,128)(2,1)}), bf16[2,2,512,512]{2,3,1,0:T(8,128)(2,1)}) %all-gather.5.cloned.1.call-update) | async-done | bytes 2097168 | tf_op jit(solution)/shard_map/while/body/eval_jaxpr/all_gather | solution.py:47
  253.5 1.8 fusion.150
  255.3 1.7 fusion.148
  259.0 5.2 collective-permute-start
  264.6 6.1 %collective-permute-done = bf16[2,2,128,512]{3,2,1,0:T(8,128)(2,1)} collective-permute-done((bf16[2,2,128,512]{3,2,1,0:T(8,128)(2,1)}, bf16[2,2,128,512]{3,2,1,0:T(8,128)(2,1)}, u32[]{:S(2)}, u32[]{:S(2)}) %collective-permute-start) | collective-permute-done | bytes 524320 | tf_op jit(solution)/shard_map/while/body/eval_jaxpr/ppermute | solution.py:16
  274.4 43.7 %all-gather.5.cloned.1.call-done = bf16[2,2,512,512]{2,3,1,0:T(8,128)(2,1)} async-done(((bf16[2,2,128,512]{2,3,1,0:T(8,128)(2,1)}), bf16[2,2,512,512]{2,3,1,0:T(8,128)(2,1)}) %all-gather.5.cloned.1.call-update) | async-done | bytes 2097168 | tf_op jit(solution)/shard_map/while/body/eval_jaxpr/all_gather | solution.py:47
  318.1 1.8 fusion.150
  319.9 1.7 fusion.148
  323.6 5.2 collective-permute-start
  329.2 6.1 %collective-permute-done = bf16[2,2,128,512]{3,2,1,0:T(8,128)(2,1)} collective-permute-done((bf16[2,2,128,512]{3,2,1,0:T(8,128)(2,1)}, bf16[2,2,128,512]{3,2,1,0:T(8,128)(2,1)}, u32[]{:S(2)}, u32[]{:S(2)}) %collective-permute-start) | collective-permute-done | bytes 524320 | tf_op jit(solution)/shard_map/while/body/eval_jaxpr/ppermute | solution.py:16
  339.0 43.7 %all-gather.5.cloned.1.call-done = bf16[2,2,512,512]{2,3,1,0:T(8,128)(2,1)} async-done(((bf16[2,2,128,512]{2,3,1,0:T(8,128)(2,1)}), bf16[2,2,512,512]{2,3,1,0:T(8,128)(2,1)}) %all-gather.5.cloned.1.call-update) | async-done | bytes 2097168 | tf_op jit(solution)/shard_map/while/body/eval_jaxpr/all_gather | solution.py:47
  382.7 1.8 fusion.150
  384.5 1.7 fusion.148
  388.2 5.2 collective-permute-start
  393.8 6.1 %collective-permute-done = bf16[2,2,128,512]{3,2,1,0:T(8,128)(2,1)} collective-permute-done((bf16[2,2,128,512]{3,2,1,0:T(8,128)(2,1)}, bf16[2,2,128,512]{3,2,1,0:T(8,128)(2,1)}, u32[]{:S(2)}, u32[]{:S(2)}) %collective-permute-start) | collective-permute-done | bytes 524320 | tf_op jit(solution)/shard_map/while/body/eval_jaxpr/ppermute | solution.py:16
  403.6 43.7 %all-gather.5.cloned.1.call-done = bf16[2,2,512,512]{2,3,1,0:T(8,128)(2,1)} async-done(((bf16[2,2,128,512]{2,3,1,0:T(8,128)(2,1)}), bf16[2,2,512,512]{2,3,1,0:T(8,128)(2,1)}) %all-gather.5.cloned.1.call-update) | async-done | bytes 2097168 | tf_op jit(solution)/shard_map/while/body/eval_jaxpr/all_gather | solution.py:47
  447.3 1.8 fusion.150
  449.1 1.7 fusion.148
  452.8 5.2 collective-permute-start
  458.4 6.1 %collective-permute-done = bf16[2,2,128,512]{3,2,1,0:T(8,128)(2,1)} collective-permute-done((bf16[2,2,128,512]{3,2,1,0:T(8,128)(2,1)}, bf16[2,2,128,512]{3,2,1,0:T(8,128)(2,1)}, u32[]{:S(2)}, u32[]{:S(2)}) %collective-permute-start) | collective-permute-done | bytes 524320 | tf_op jit(solution)/shard_map/while/body/eval_jaxpr/ppermute | solution.py:16
  468.2 43.7 %all-gather.5.cloned.1.call-done = bf16[2,2,512,512]{2,3,1,0:T(8,128)(2,1)} async-done(((bf16[2,2,128,512]{2,3,1,0:T(8,128)(2,1)}), bf16[2,2,512,512]{2,3,1,0:T(8,128)(2,1)}) %all-gather.5.cloned.1.call-update) | async-done | bytes 2097168 | tf_op jit(solution)/shard_map/while/body/eval_jaxpr/all_gather | solution.py:47
  511.9 1.8 fusion.150
  513.7 1.7 fusion.148
  516.8 5.4 collective-permute-start.1
  522.2 1.9 collective-permute-start.2
  524.8 3.5 collective-permute-done.1
  528.3 7.2 %collective-permute-done.2 = bf16[2,1,2,128,512]{4,3,2,1,0:T(8,128)(2,1)S(1)} collective-permute-done((bf16[2,1,2,128,512]{4,3,2,1,0:T(8,128)(2,1)S(1)}, bf16[2,1,2,128,512]{4,3,2,1,0:T(8,128)(2,1)S(1)}, u32[]{:S(2)}, u32[]{:S(2)}) %collective-permute-start.2) | collective-permute-done | bytes 524320 | tf_op jit(solution)/shard_map/ppermute | solution.py:29
  535.6 1.3 collective-permute-start.3
  536.9 1.3 collective-permute-start.4
  538.2 3.2 collective-permute-done.4
  542.0 5.4 fusion.68
  (177 shorter events, 50.5 us)
Async XLA Ops:
  7.2 1.5 copy-start
  7.2 52.6 %all-gather.3.cloned.1.call-start = ((), (), s32[]{:S(2)}) async-start(), calls=%async_computation | async-start | bytes 2621440 | tf_op jit(solution)/shard_map/all_gather | solution.py:47
  9.6 3.2 copy-start.4
  10.8 48.9 %copy-start.2 = (bf16[1,2,128,512]{3,2,1,0:T(8,128)(2,1)S(1)}, bf16[1,2,128,512]{3,2,1,0:T(8,128)(2,1)}, u32[]{:S(2)}) copy-start(bf16[1,2,128,512]{3,2,1,0:T(8,128)(2,1)} %param.11) | copy-start | bytes 786436
  59.7 3.5 copy-start.7
  64.2 60.2 %all-gather.5.cloned.1.call-start = ((), (), s32[]{:S(2)}) async-start(), calls=%async_computation.1 | async-start | bytes 2621440 | tf_op jit(solution)/shard_map/while/body/eval_jaxpr/all_gather | solution.py:47
  65.2 11.7 %collective-permute-start = (bf16[2,2,128,512]{3,2,1,0:T(8,128)(2,1)}, bf16[2,2,128,512]{3,2,1,0:T(8,128)(2,1)}, u32[]{:S(2)}, u32[]{:S(2)}) collective-permute-start(bf16[2,2,128,512]{3,2,1,0:T(8,128)(2,1)} %bitcast.168), channel_id=1, source_target_pairs={{0,4},{4,8},{8,12},{12,16},{16,20},{20,24},{24,28},{1,5},{5,9},{9,... | collective-permute-start | bytes 1572872 | tf_op jit(solution)/shard_map/while/body/eval_jaxpr/ppermute | solution.py:16
  79.5 44.8 %copy-start.3 = (bf16[1,2,128,512]{3,2,1,0:T(8,128)(2,1)S(1)}, bf16[1,2,128,512]{3,2,1,0:T(8,128)(2,1)}, u32[]{:S(2)}) copy-start(bf16[1,2,128,512]{3,2,1,0:T(8,128)(2,1)} %get-tuple-element.113) | copy-start | bytes 786436 | tf_op jit(solution)/shard_map/while
  124.3 3.5 copy-start.1
  128.8 60.2 %all-gather.5.cloned.1.call-start = ((), (), s32[]{:S(2)}) async-start(), calls=%async_computation.1 | async-start | bytes 2621440 | tf_op jit(solution)/shard_map/while/body/eval_jaxpr/all_gather | solution.py:47
  129.8 11.7 %collective-permute-start = (bf16[2,2,128,512]{3,2,1,0:T(8,128)(2,1)}, bf16[2,2,128,512]{3,2,1,0:T(8,128)(2,1)}, u32[]{:S(2)}, u32[]{:S(2)}) collective-permute-start(bf16[2,2,128,512]{3,2,1,0:T(8,128)(2,1)} %bitcast.168), channel_id=1, source_target_pairs={{0,4},{4,8},{8,12},{12,16},{16,20},{20,24},{24,28},{1,5},{5,9},{9,... | collective-permute-start | bytes 1572872 | tf_op jit(solution)/shard_map/while/body/eval_jaxpr/ppermute | solution.py:16
  144.1 44.8 %copy-start.3 = (bf16[1,2,128,512]{3,2,1,0:T(8,128)(2,1)S(1)}, bf16[1,2,128,512]{3,2,1,0:T(8,128)(2,1)}, u32[]{:S(2)}) copy-start(bf16[1,2,128,512]{3,2,1,0:T(8,128)(2,1)} %get-tuple-element.113) | copy-start | bytes 786436 | tf_op jit(solution)/shard_map/while
  188.9 3.5 copy-start.1
  193.4 60.2 %all-gather.5.cloned.1.call-start = ((), (), s32[]{:S(2)}) async-start(), calls=%async_computation.1 | async-start | bytes 2621440 | tf_op jit(solution)/shard_map/while/body/eval_jaxpr/all_gather | solution.py:47
  194.4 11.7 %collective-permute-start = (bf16[2,2,128,512]{3,2,1,0:T(8,128)(2,1)}, bf16[2,2,128,512]{3,2,1,0:T(8,128)(2,1)}, u32[]{:S(2)}, u32[]{:S(2)}) collective-permute-start(bf16[2,2,128,512]{3,2,1,0:T(8,128)(2,1)} %bitcast.168), channel_id=1, source_target_pairs={{0,4},{4,8},{8,12},{12,16},{16,20},{20,24},{24,28},{1,5},{5,9},{9,... | collective-permute-start | bytes 1572872 | tf_op jit(solution)/shard_map/while/body/eval_jaxpr/ppermute | solution.py:16
  208.7 44.8 %copy-start.3 = (bf16[1,2,128,512]{3,2,1,0:T(8,128)(2,1)S(1)}, bf16[1,2,128,512]{3,2,1,0:T(8,128)(2,1)}, u32[]{:S(2)}) copy-start(bf16[1,2,128,512]{3,2,1,0:T(8,128)(2,1)} %get-tuple-element.113) | copy-start | bytes 786436 | tf_op jit(solution)/shard_map/while
  253.5 3.5 copy-start.1
  258.0 60.2 %all-gather.5.cloned.1.call-start = ((), (), s32[]{:S(2)}) async-start(), calls=%async_computation.1 | async-start | bytes 2621440 | tf_op jit(solution)/shard_map/while/body/eval_jaxpr/all_gather | solution.py:47
  259.0 11.7 %collective-permute-start = (bf16[2,2,128,512]{3,2,1,0:T(8,128)(2,1)}, bf16[2,2,128,512]{3,2,1,0:T(8,128)(2,1)}, u32[]{:S(2)}, u32[]{:S(2)}) collective-permute-start(bf16[2,2,128,512]{3,2,1,0:T(8,128)(2,1)} %bitcast.168), channel_id=1, source_target_pairs={{0,4},{4,8},{8,12},{12,16},{16,20},{20,24},{24,28},{1,5},{5,9},{9,... | collective-permute-start | bytes 1572872 | tf_op jit(solution)/shard_map/while/body/eval_jaxpr/ppermute | solution.py:16
  273.3 44.8 %copy-start.3 = (bf16[1,2,128,512]{3,2,1,0:T(8,128)(2,1)S(1)}, bf16[1,2,128,512]{3,2,1,0:T(8,128)(2,1)}, u32[]{:S(2)}) copy-start(bf16[1,2,128,512]{3,2,1,0:T(8,128)(2,1)} %get-tuple-element.113) | copy-start | bytes 786436 | tf_op jit(solution)/shard_map/while
  318.1 3.5 copy-start.1
  322.6 60.2 %all-gather.5.cloned.1.call-start = ((), (), s32[]{:S(2)}) async-start(), calls=%async_computation.1 | async-start | bytes 2621440 | tf_op jit(solution)/shard_map/while/body/eval_jaxpr/all_gather | solution.py:47
  323.6 11.7 %collective-permute-start = (bf16[2,2,128,512]{3,2,1,0:T(8,128)(2,1)}, bf16[2,2,128,512]{3,2,1,0:T(8,128)(2,1)}, u32[]{:S(2)}, u32[]{:S(2)}) collective-permute-start(bf16[2,2,128,512]{3,2,1,0:T(8,128)(2,1)} %bitcast.168), channel_id=1, source_target_pairs={{0,4},{4,8},{8,12},{12,16},{16,20},{20,24},{24,28},{1,5},{5,9},{9,... | collective-permute-start | bytes 1572872 | tf_op jit(solution)/shard_map/while/body/eval_jaxpr/ppermute | solution.py:16
  337.9 44.8 %copy-start.3 = (bf16[1,2,128,512]{3,2,1,0:T(8,128)(2,1)S(1)}, bf16[1,2,128,512]{3,2,1,0:T(8,128)(2,1)}, u32[]{:S(2)}) copy-start(bf16[1,2,128,512]{3,2,1,0:T(8,128)(2,1)} %get-tuple-element.113) | copy-start | bytes 786436 | tf_op jit(solution)/shard_map/while
  382.7 3.5 copy-start.1
  387.2 60.2 %all-gather.5.cloned.1.call-start = ((), (), s32[]{:S(2)}) async-start(), calls=%async_computation.1 | async-start | bytes 2621440 | tf_op jit(solution)/shard_map/while/body/eval_jaxpr/all_gather | solution.py:47
  388.2 11.7 %collective-permute-start = (bf16[2,2,128,512]{3,2,1,0:T(8,128)(2,1)}, bf16[2,2,128,512]{3,2,1,0:T(8,128)(2,1)}, u32[]{:S(2)}, u32[]{:S(2)}) collective-permute-start(bf16[2,2,128,512]{3,2,1,0:T(8,128)(2,1)} %bitcast.168), channel_id=1, source_target_pairs={{0,4},{4,8},{8,12},{12,16},{16,20},{20,24},{24,28},{1,5},{5,9},{9,... | collective-permute-start | bytes 1572872 | tf_op jit(solution)/shard_map/while/body/eval_jaxpr/ppermute | solution.py:16
  402.5 44.8 %copy-start.3 = (bf16[1,2,128,512]{3,2,1,0:T(8,128)(2,1)S(1)}, bf16[1,2,128,512]{3,2,1,0:T(8,128)(2,1)}, u32[]{:S(2)}) copy-start(bf16[1,2,128,512]{3,2,1,0:T(8,128)(2,1)} %get-tuple-element.113) | copy-start | bytes 786436 | tf_op jit(solution)/shard_map/while
  447.3 3.5 copy-start.1
  451.8 60.2 %all-gather.5.cloned.1.call-start = ((), (), s32[]{:S(2)}) async-start(), calls=%async_computation.1 | async-start | bytes 2621440 | tf_op jit(solution)/shard_map/while/body/eval_jaxpr/all_gather | solution.py:47
  452.8 11.7 %collective-permute-start = (bf16[2,2,128,512]{3,2,1,0:T(8,128)(2,1)}, bf16[2,2,128,512]{3,2,1,0:T(8,128)(2,1)}, u32[]{:S(2)}, u32[]{:S(2)}) collective-permute-start(bf16[2,2,128,512]{3,2,1,0:T(8,128)(2,1)} %bitcast.168), channel_id=1, source_target_pairs={{0,4},{4,8},{8,12},{12,16},{16,20},{20,24},{24,28},{1,5},{5,9},{9,... | collective-permute-start | bytes 1572872 | tf_op jit(solution)/shard_map/while/body/eval_jaxpr/ppermute | solution.py:16
  467.1 44.8 %copy-start.3 = (bf16[1,2,128,512]{3,2,1,0:T(8,128)(2,1)S(1)}, bf16[1,2,128,512]{3,2,1,0:T(8,128)(2,1)}, u32[]{:S(2)}) copy-start(bf16[1,2,128,512]{3,2,1,0:T(8,128)(2,1)} %get-tuple-element.113) | copy-start | bytes 786436 | tf_op jit(solution)/shard_map/while
  511.9 3.5 copy-start.1
  516.7 30.7 %copy-start.6 = (f32[2,1,2,128,512]{4,3,2,1,0:T(8,128)}, f32[2,1,2,128,512]{4,3,2,1,0:T(8,128)S(1)}, u32[]{:S(2)}) copy-start(f32[2,1,2,128,512]{4,3,2,1,0:T(8,128)S(1)} %copy.26) | copy-start | bytes 3145732
  516.7 21.5 %copy-start.8 = (f32[1,128,512]{2,1,0:T(8,128)S(1)}, f32[1,128,512]{2,1,0:T(8,128)}, u32[]{:S(2)}) copy-start(f32[1,128,512]{2,1,0:T(8,128)} %param.8) | copy-start | bytes 786436
  516.8 11.5 %collective-permute-start.1 = (bf16[2,1,2,128,512]{4,3,2,1,0:T(8,128)(2,1)S(1)}, bf16[2,1,2,128,512]{4,3,2,1,0:T(8,128)(2,1)S(1)}, u32[]{:S(2)}, u32[]{:S(2)}) collective-permute-start(bf16[2,1,2,128,512]{4,3,2,1,0:T(8,128)(2,1)S(1)} %convert_element_type.40), channel_id=1, source_target_pairs={{0,4},{4,8},{8,12},{12,16},{16,20},{20,24},{24,28},{1,5},{5,9},{9,... | collective-permute-start | bytes 1572872 | tf_op jit(solution)/shard_map/ppermute | solution.py:27
  522.2 13.3 %collective-permute-start.2 = (bf16[2,1,2,128,512]{4,3,2,1,0:T(8,128)(2,1)S(1)}, bf16[2,1,2,128,512]{4,3,2,1,0:T(8,128)(2,1)S(1)}, u32[]{:S(2)}, u32[]{:S(2)}) collective-permute-start(bf16[2,1,2,128,512]{4,3,2,1,0:T(8,128)(2,1)S(1)} %convert_element_type.40), channel_id=1, source_target_pairs={{4,0},{8,4},{12,8},{16,12},{20,16},{24,20},{28,24},{5,1},{9,5},{13... | collective-permute-start | bytes 1572872 | tf_op jit(solution)/shard_map/ppermute | solution.py:29
  535.6 2.6 collective-permute-start.3
  536.9 4.6 collective-permute-start.4
  547.4 1.2 copy-start.5
Sparse Core Ops, SparseCore 0:
  13.0 46.7 all-gather.2
  80.7 43.5 all-gather.4
  145.3 43.5 all-gather.4
  209.9 43.5 all-gather.4
  274.5 43.5 all-gather.4
  339.1 43.5 all-gather.4
  403.7 43.5 all-gather.4
  468.3 43.5 all-gather.4
where the time goes:
time: 558 us; the launch traced here: 557 us
  waiting for transfers between devices  409 us (73%)
  starting transfers between devices  46.9 us (8%)
  matrix products  44.8 us (8%)
  other arithmetic  24.7 us (4%)
  local copies, waits for them, and re-layouts  15 us (3%)
  between operations  14.9 us (3%)
    all_gather x8, waiting for transfers between devices, cross_fold(): gathered = lax.all_gather(mixed, 'cross', axis=2, tiled=True)  353 us
    ppermute x7, waiting for transfers between devices, passed_along(): return lax.ppermute(shard, axis, pairs)  42.6 us
    ppermute x7, starting transfers between devices, passed_along(): return lax.ppermute(shard, axis, pairs)  36.7 us
    dot_general x8, matrix products, cross_fold(): jnp.einsum('yk,rkx->ryx', coupling_rows[0], gathered[0], preferred_elemen...  14.4 us
    dot_general x8, matrix products, cross_fold(): jnp.einsum('yk,rkx->ryx', coupling_rows[0], gathered[1], preferred_elemen...  13.2 us
  transfers between devices with their start and end apart: 19, of which 18 were waited for; matrix products, arithmetic and copies ran while one was open for 0% of the time, Pallas kernels for 0%

commit v1 on v0

--- a/solution.py
+++ b/solution.py
@@ -8,6 +8,12 @@
 FACE = 14.0 / 30.0
 EDGE = 3.0 / 30.0
 CORNER = 1.0 / 30.0
+
+
+def joined_along(blocks, dim):
+    shape = list(blocks.shape[1:])
+    shape[dim] *= blocks.shape[0]
+    return jnp.moveaxis(blocks, 0, dim).reshape(shape)
 
 
 def passed_along(shard, axis, by):
@@ -44,7 +50,14 @@
 
 
 def cross_fold(mixed, coupling_rows):
-    gathered = lax.all_gather(mixed, "cross", axis=2, tiled=True)
+    size = lax.axis_size("cross")
+    right = [(i_2, (i_2 + 1) % size) for i_2 in range(size)]
+    blocks = [mixed]
+    while len(blocks) < size:
+        blocks.append(lax.ppermute(blocks[-1], "cross", right))
+    here = lax.axis_index("cross")
+    blocks = jnp.stack(blocks)[(here - jnp.arange(size)) % size]
+    gathered = joined_along(blocks, 2)
     real_real = jnp.einsum(
         "yk,rkx->ryx", coupling_rows[0], gathered[0], preferred_element_type=jnp.float32
     )

time: 558 us -> 598 us (1.072)
  local copies, waits for them, and re-layouts: 15 us -> 106 us
  waiting for transfers between devices: 409 us -> 333 us
  starting transfers between devices: 46.9 us -> 96.7 us
  matrix products: 44.8 us -> 24.7 us
  between operations: 14.9 us -> 1.57 us
  other arithmetic: 24.7 us -> 33.4 us
    all_gather x8 -> x0, waiting for transfers between devices: 353 us -> none  [cross_fold(): gathered = lax.all_gather(mixed, 'cross', axis=2, tiled=True)]
    ppermute x0 -> x24, waiting for transfers between devices: none -> 281 us  [cross_fold(): blocks.append(lax.ppermute(blocks[-1], 'cross', right))]
    slice x0 -> x24, local copies, waits for them, and re-layouts: none -> 48.4 us  [the longest x16 28.8 us: cross_fold(): gathered[0]]
    ppermute x7, starting transfers between devices: 36.7 us -> 67.9 us  [passed_along(): return lax.ppermute(shard, axis, pairs)]
    gather x0 -> x8, local copies, waits for them, and re-layouts: none -> 17.8 us  [cross_fold(): blocks = jnp.stack(blocks)[(here - jnp.arange(size)) % size]]
    squeeze x0 -> x16, local copies, waits for them, and re-layouts: none -> 16.8 us  [the longest x8 12.5 us: cross_fold(): gathered[1]]
    ppermute x2, starting transfers between devices: 6.67 us -> 22.9 us  [with_halo(): lax.ppermute(tail, axis, [(i, (i + 1) % count) for i in range(ends)])]
    another operation x0 -> x8, other arithmetic: none -> 14.8 us  [cross_fold(): blocks = jnp.stack(blocks)[(here - jnp.arange(size)) % size]]
  transfers between devices with their start and end apart: 19 -> 35, of which waited for: 18 -> 34; matrix products, arithmetic and copies ran while one was open for 0% -> 0% of each run, Pallas kernels for 0% -> 0%
where the time goes in v1:
time: 598 us; the launch traced here: 596 us
  waiting for transfers between devices  333 us (56%)
  local copies, waits for them, and re-layouts  106 us (18%)
  starting transfers between devices  96.7 us (16%)
  other arithmetic  33.4 us (6%)
  matrix products  24.7 us (4%)
    ppermute x24, waiting for transfers between devices, cross_fold(): blocks.append(lax.ppermute(blocks[-1], 'cross', right))  281 us
    ppermute x7, starting transfers between devices, passed_along(): return lax.ppermute(shard, axis, pairs)  67.9 us
    ppermute x7, waiting for transfers between devices, passed_along(): return lax.ppermute(shard, axis, pairs)  42.6 us
    slice x16, local copies, waits for them, and re-layouts, cross_fold(): gathered[0]  28.8 us
    ppermute x2, starting transfers between devices, with_halo(): lax.ppermute(tail, axis, [(i, (i + 1) % count) for i in range(ends)])  22.9 us
    slice x8, local copies, waits for them, and re-layouts, cross_fold(): gathered[1]  19.5 us
    gather x8, local copies, waits for them, and re-layouts, cross_fold(): blocks = jnp.stack(blocks)[(here - jnp.arange(size)) % size]  17.8 us
    another operation x8, other arithmetic, cross_fold(): blocks = jnp.stack(blocks)[(here - jnp.arange(size)) % size]  14.8 us
  transfers between devices with their start and end apart: 35, of which 34 were waited for; matrix products, arithmetic and copies ran while one was open for 0% of the time, Pallas kernels for 0%

profile of v1, /device:TPU:1, one launch (start us, length us, event | category | flops | bytes accessed | tf_op | source)
XLA Modules:
  0.0 596.3 jit_solution(679386072344173122)
XLA Ops:
  5.6 13.6 %collective-permute-done.4 = bf16[2,2,128,512]{3,2,1,0:T(8,128)(2,1)S(1)} collective-permute-done((bf16[2,2,128,512]{3,2,1,0:T(8,128)(2,1)S(1)}, bf16[2,2,128,512]{3,2,1,0:T(8,128)(2,1)S(1)}, u32[]{:S(2)}, u32[]{:S(2)}) %collective-permute-start.4) | collective-permute-done | bytes 524320 | tf_op jit(solution)/shard_map/ppermute | solution.py:57
  19.3 14.1 %collective-permute-done.5 = bf16[2,2,128,512]{3,2,1,0:T(8,128)(2,1)} collective-permute-done((bf16[2,2,128,512]{3,2,1,0:T(8,128)(2,1)S(1)}, bf16[2,2,128,512]{3,2,1,0:T(8,128)(2,1)}, u32[]{:S(2)}, u32[]{:S(2)}) %collective-permute-start.5) | collective-permute-done | bytes 524320 | tf_op jit(solution)/shard_map/ppermute | solution.py:57
  33.8 13.1 %collective-permute-done.6 = bf16[2,2,128,512]{3,2,1,0:T(8,128)(2,1)} collective-permute-done((bf16[2,2,128,512]{3,2,1,0:T(8,128)(2,1)}, bf16[2,2,128,512]{3,2,1,0:T(8,128)(2,1)}, u32[]{:S(2)}, u32[]{:S(2)}) %collective-permute-start.6) | collective-permute-done | bytes 524320 | tf_op jit(solution)/shard_map/ppermute | solution.py:57
  46.9 3.0 pad_maximum_fusion.2
  49.9 3.6 gather_fusion.1
  53.5 3.0 fusion.104
  67.7 483.7 %while.12 = (s32[]{:T(128)}, f32[2,1,2,128,512]{3,4,2,0,1:T(8,128)S(1)}, f32[2,1,2,128,512]{3,4,2,0,1:T(8,128)S(1)}, bf16[2,512,512]{2,1,0:T(8,128)(2,1)S(1)}, b...) while((s32[]{:T(128)}, f32[2,1,2,128,512]{3,4,2,0,1:T(8,128)S(1)}, ...), condition=%wide.region_1.2_spmd, body=%wide.region_0.1_spmd.sunk | while | flops 1080034304 | bytes 69734904 | solution.py:144
  68.9 5.5 collective-permute-start
  74.7 6.1 %collective-permute-done = bf16[2,2,128,512]{3,2,1,0:T(8,128)(2,1)} collective-permute-done((bf16[2,2,128,512]{3,2,1,0:T(8,128)(2,1)}, bf16[2,2,128,512]{3,2,1,0:T(8,128)(2,1)}, u32[]{:S(2)}, u32[]{:S(2)}) %collective-permute-start) | collective-permute-done | bytes 524320 | tf_op jit(solution)/shard_map/while/body/eval_jaxpr/ppermute | solution.py:22
  83.4 10.4 %collective-permute-done.1 = bf16[2,2,128,512]{3,2,1,0:T(8,128)(2,1)S(1)} collective-permute-done((bf16[2,2,128,512]{3,2,1,0:T(8,128)(2,1)S(1)}, bf16[2,2,128,512]{3,2,1,0:T(8,128)(2,1)S(1)}, u32[]{:S(2)}, u32[]{:S(2)}) %collective-permute-start.1) | collective-permute-done | bytes 524320 | tf_op jit(solution)/shard_map/while/body/eval_jaxpr/ppermute | solution.py:57
  93.8 10.9 %collective-permute-done.2 = bf16[2,2,128,512]{3,2,1,0:T(8,128)(2,1)S(1)} collective-permute-done((bf16[2,2,128,512]{3,2,1,0:T(8,128)(2,1)S(1)}, bf16[2,2,128,512]{3,2,1,0:T(8,128)(2,1)S(1)}, u32[]{:S(2)}, u32[]{:S(2)}) %collective-permute-start.2) | collective-permute-done | bytes 524320 | tf_op jit(solution)/shard_map/while/body/eval_jaxpr/ppermute | solution.py:57
  104.8 12.0 %collective-permute-done.3 = bf16[2,2,128,512]{3,2,1,0:T(8,128)(2,1)S(1)} collective-permute-done((bf16[2,2,128,512]{3,2,1,0:T(8,128)(2,1)S(1)}, bf16[2,2,128,512]{3,2,1,0:T(8,128)(2,1)S(1)}, u32[]{:S(2)}, u32[]{:S(2)}) %collective-permute-start.3) | collective-permute-done | bytes 524320 | tf_op jit(solution)/shard_map/while/body/eval_jaxpr/ppermute | solution.py:57
  132.8 12.7 %collective-permute-start = (bf16[2,2,128,512]{3,2,1,0:T(8,128)(2,1)}, bf16[2,2,128,512]{3,2,1,0:T(8,128)(2,1)}, u32[]{:S(2)}, u32[]{:S(2)}) collective-permute-start(bf16[2,2,128,512]{3,2,1,0:T(8,128)(2,1)} %bitcast.201), channel_id=1, source_target_pairs={{0,4},{4,8},{8,12},{12,16},{16,20},{20,24},{24,28},{1,5},{5,9},{9,... | collective-permute-start | bytes 1572872 | tf_op jit(solution)/shard_map/while/body/eval_jaxpr/ppermute | solution.py:22
  145.9 6.1 %collective-permute-done = bf16[2,2,128,512]{3,2,1,0:T(8,128)(2,1)} collective-permute-done((bf16[2,2,128,512]{3,2,1,0:T(8,128)(2,1)}, bf16[2,2,128,512]{3,2,1,0:T(8,128)(2,1)}, u32[]{:S(2)}, u32[]{:S(2)}) %collective-permute-start) | collective-permute-done | bytes 524320 | tf_op jit(solution)/shard_map/while/body/eval_jaxpr/ppermute | solution.py:22
  154.6 12.0 %collective-permute-done.1 = bf16[2,2,128,512]{3,2,1,0:T(8,128)(2,1)S(1)} collective-permute-done((bf16[2,2,128,512]{3,2,1,0:T(8,128)(2,1)S(1)}, bf16[2,2,128,512]{3,2,1,0:T(8,128)(2,1)S(1)}, u32[]{:S(2)}, u32[]{:S(2)}) %collective-permute-start.1) | collective-permute-done | bytes 524320 | tf_op jit(solution)/shard_map/while/body/eval_jaxpr/ppermute | solution.py:57
  166.6 13.2 %collective-permute-done.2 = bf16[2,2,128,512]{3,2,1,0:T(8,128)(2,1)S(1)} collective-permute-done((bf16[2,2,128,512]{3,2,1,0:T(8,128)(2,1)S(1)}, bf16[2,2,128,512]{3,2,1,0:T(8,128)(2,1)S(1)}, u32[]{:S(2)}, u32[]{:S(2)}) %collective-permute-start.2) | collective-permute-done | bytes 524320 | tf_op jit(solution)/shard_map/while/body/eval_jaxpr/ppermute | solution.py:57
  179.8 9.8 %collective-permute-done.3 = bf16[2,2,128,512]{3,2,1,0:T(8,128)(2,1)S(1)} collective-permute-done((bf16[2,2,128,512]{3,2,1,0:T(8,128)(2,1)S(1)}, bf16[2,2,128,512]{3,2,1,0:T(8,128)(2,1)S(1)}, u32[]{:S(2)}, u32[]{:S(2)}) %collective-permute-start.3) | collective-permute-done | bytes 524320 | tf_op jit(solution)/shard_map/while/body/eval_jaxpr/ppermute | solution.py:57
  194.1 2.7 fusion.173
  205.6 5.6 collective-permute-start
  211.6 6.1 %collective-permute-done = bf16[2,2,128,512]{3,2,1,0:T(8,128)(2,1)} collective-permute-done((bf16[2,2,128,512]{3,2,1,0:T(8,128)(2,1)}, bf16[2,2,128,512]{3,2,1,0:T(8,128)(2,1)}, u32[]{:S(2)}, u32[]{:S(2)}) %collective-permute-start) | collective-permute-done | bytes 524320 | tf_op jit(solution)/shard_map/while/body/eval_jaxpr/ppermute | solution.py:22
  220.3 12.1 %collective-permute-done.1 = bf16[2,2,128,512]{3,2,1,0:T(8,128)(2,1)S(1)} collective-permute-done((bf16[2,2,128,512]{3,2,1,0:T(8,128)(2,1)S(1)}, bf16[2,2,128,512]{3,2,1,0:T(8,128)(2,1)S(1)}, u32[]{:S(2)}, u32[]{:S(2)}) %collective-permute-start.1) | collective-permute-done | bytes 524320 | tf_op jit(solution)/shard_map/while/body/eval_jaxpr/ppermute | solution.py:57
  232.4 11.2 %collective-permute-done.2 = bf16[2,2,128,512]{3,2,1,0:T(8,128)(2,1)S(1)} collective-permute-done((bf16[2,2,128,512]{3,2,1,0:T(8,128)(2,1)S(1)}, bf16[2,2,128,512]{3,2,1,0:T(8,128)(2,1)S(1)}, u32[]{:S(2)}, u32[]{:S(2)}) %collective-permute-start.2) | collective-permute-done | bytes 524320 | tf_op jit(solution)/shard_map/while/body/eval_jaxpr/ppermute | solution.py:57
  243.7 9.8 %collective-permute-done.3 = bf16[2,2,128,512]{3,2,1,0:T(8,128)(2,1)S(1)} collective-permute-done((bf16[2,2,128,512]{3,2,1,0:T(8,128)(2,1)S(1)}, bf16[2,2,128,512]{3,2,1,0:T(8,128)(2,1)S(1)}, u32[]{:S(2)}, u32[]{:S(2)}) %collective-permute-start.3) | collective-permute-done | bytes 524320 | tf_op jit(solution)/shard_map/while/body/eval_jaxpr/ppermute | solution.py:57
  269.5 15.5 %collective-permute-start = (bf16[2,2,128,512]{3,2,1,0:T(8,128)(2,1)}, bf16[2,2,128,512]{3,2,1,0:T(8,128)(2,1)}, u32[]{:S(2)}, u32[]{:S(2)}) collective-permute-start(bf16[2,2,128,512]{3,2,1,0:T(8,128)(2,1)} %bitcast.201), channel_id=1, source_target_pairs={{0,4},{4,8},{8,12},{12,16},{16,20},{20,24},{24,28},{1,5},{5,9},{9,... | collective-permute-start | bytes 1572872 | tf_op jit(solution)/shard_map/while/body/eval_jaxpr/ppermute | solution.py:22
  285.4 6.1 %collective-permute-done = bf16[2,2,128,512]{3,2,1,0:T(8,128)(2,1)} collective-permute-done((bf16[2,2,128,512]{3,2,1,0:T(8,128)(2,1)}, bf16[2,2,128,512]{3,2,1,0:T(8,128)(2,1)}, u32[]{:S(2)}, u32[]{:S(2)}) %collective-permute-start) | collective-permute-done | bytes 524320 | tf_op jit(solution)/shard_map/while/body/eval_jaxpr/ppermute | solution.py:22
  294.1 11.0 %collective-permute-done.1 = bf16[2,2,128,512]{3,2,1,0:T(8,128)(2,1)S(1)} collective-permute-done((bf16[2,2,128,512]{3,2,1,0:T(8,128)(2,1)S(1)}, bf16[2,2,128,512]{3,2,1,0:T(8,128)(2,1)S(1)}, u32[]{:S(2)}, u32[]{:S(2)}) %collective-permute-start.1) | collective-permute-done | bytes 524320 | tf_op jit(solution)/shard_map/while/body/eval_jaxpr/ppermute | solution.py:57
  305.1 10.1 %collective-permute-done.2 = bf16[2,2,128,512]{3,2,1,0:T(8,128)(2,1)S(1)} collective-permute-done((bf16[2,2,128,512]{3,2,1,0:T(8,128)(2,1)S(1)}, bf16[2,2,128,512]{3,2,1,0:T(8,128)(2,1)S(1)}, u32[]{:S(2)}, u32[]{:S(2)}) %collective-permute-start.2) | collective-permute-done | bytes 524320 | tf_op jit(solution)/shard_map/while/body/eval_jaxpr/ppermute | solution.py:57
  315.2 9.8 %collective-permute-done.3 = bf16[2,2,128,512]{3,2,1,0:T(8,128)(2,1)S(1)} collective-permute-done((bf16[2,2,128,512]{3,2,1,0:T(8,128)(2,1)S(1)}, bf16[2,2,128,512]{3,2,1,0:T(8,128)(2,1)S(1)}, u32[]{:S(2)}, u32[]{:S(2)}) %collective-permute-start.3) | collective-permute-done | bytes 524320 | tf_op jit(solution)/shard_map/while/body/eval_jaxpr/ppermute | solution.py:57
  341.0 11.8 %collective-permute-start = (bf16[2,2,128,512]{3,2,1,0:T(8,128)(2,1)}, bf16[2,2,128,512]{3,2,1,0:T(8,128)(2,1)}, u32[]{:S(2)}, u32[]{:S(2)}) collective-permute-start(bf16[2,2,128,512]{3,2,1,0:T(8,128)(2,1)} %bitcast.201), channel_id=1, source_target_pairs={{0,4},{4,8},{8,12},{12,16},{16,20},{20,24},{24,28},{1,5},{5,9},{9,... | collective-permute-start | bytes 1572872 | tf_op jit(solution)/shard_map/while/body/eval_jaxpr/ppermute | solution.py:22
  353.2 6.1 %collective-permute-done = bf16[2,2,128,512]{3,2,1,0:T(8,128)(2,1)} collective-permute-done((bf16[2,2,128,512]{3,2,1,0:T(8,128)(2,1)}, bf16[2,2,128,512]{3,2,1,0:T(8,128)(2,1)}, u32[]{:S(2)}, u32[]{:S(2)}) %collective-permute-start) | collective-permute-done | bytes 524320 | tf_op jit(solution)/shard_map/while/body/eval_jaxpr/ppermute | solution.py:22
  361.9 12.9 %collective-permute-done.1 = bf16[2,2,128,512]{3,2,1,0:T(8,128)(2,1)S(1)} collective-permute-done((bf16[2,2,128,512]{3,2,1,0:T(8,128)(2,1)S(1)}, bf16[2,2,128,512]{3,2,1,0:T(8,128)(2,1)S(1)}, u32[]{:S(2)}, u32[]{:S(2)}) %collective-permute-start.1) | collective-permute-done | bytes 524320 | tf_op jit(solution)/shard_map/while/body/eval_jaxpr/ppermute | solution.py:57
  374.8 14.0 %collective-permute-done.2 = bf16[2,2,128,512]{3,2,1,0:T(8,128)(2,1)S(1)} collective-permute-done((bf16[2,2,128,512]{3,2,1,0:T(8,128)(2,1)S(1)}, bf16[2,2,128,512]{3,2,1,0:T(8,128)(2,1)S(1)}, u32[]{:S(2)}, u32[]{:S(2)}) %collective-permute-start.2) | collective-permute-done | bytes 524320 | tf_op jit(solution)/shard_map/while/body/eval_jaxpr/ppermute | solution.py:57
  388.8 9.8 %collective-permute-done.3 = bf16[2,2,128,512]{3,2,1,0:T(8,128)(2,1)S(1)} collective-permute-done((bf16[2,2,128,512]{3,2,1,0:T(8,128)(2,1)S(1)}, bf16[2,2,128,512]{3,2,1,0:T(8,128)(2,1)S(1)}, u32[]{:S(2)}, u32[]{:S(2)}) %collective-permute-start.3) | collective-permute-done | bytes 524320 | tf_op jit(solution)/shard_map/while/body/eval_jaxpr/ppermute | solution.py:57
  414.7 11.2 %collective-permute-start = (bf16[2,2,128,512]{3,2,1,0:T(8,128)(2,1)}, bf16[2,2,128,512]{3,2,1,0:T(8,128)(2,1)}, u32[]{:S(2)}, u32[]{:S(2)}) collective-permute-start(bf16[2,2,128,512]{3,2,1,0:T(8,128)(2,1)} %bitcast.201), channel_id=1, source_target_pairs={{0,4},{4,8},{8,12},{12,16},{16,20},{20,24},{24,28},{1,5},{5,9},{9,... | collective-permute-start | bytes 1572872 | tf_op jit(solution)/shard_map/while/body/eval_jaxpr/ppermute | solution.py:22
  426.2 6.1 %collective-permute-done = bf16[2,2,128,512]{3,2,1,0:T(8,128)(2,1)} collective-permute-done((bf16[2,2,128,512]{3,2,1,0:T(8,128)(2,1)}, bf16[2,2,128,512]{3,2,1,0:T(8,128)(2,1)}, u32[]{:S(2)}, u32[]{:S(2)}) %collective-permute-start) | collective-permute-done | bytes 524320 | tf_op jit(solution)/shard_map/while/body/eval_jaxpr/ppermute | solution.py:22
  434.9 13.5 %collective-permute-done.1 = bf16[2,2,128,512]{3,2,1,0:T(8,128)(2,1)S(1)} collective-permute-done((bf16[2,2,128,512]{3,2,1,0:T(8,128)(2,1)S(1)}, bf16[2,2,128,512]{3,2,1,0:T(8,128)(2,1)S(1)}, u32[]{:S(2)}, u32[]{:S(2)}) %collective-permute-start.1) | collective-permute-done | bytes 524320 | tf_op jit(solution)/shard_map/while/body/eval_jaxpr/ppermute | solution.py:57
  448.4 14.7 %collective-permute-done.2 = bf16[2,2,128,512]{3,2,1,0:T(8,128)(2,1)S(1)} collective-permute-done((bf16[2,2,128,512]{3,2,1,0:T(8,128)(2,1)S(1)}, bf16[2,2,128,512]{3,2,1,0:T(8,128)(2,1)S(1)}, u32[]{:S(2)}, u32[]{:S(2)}) %collective-permute-start.2) | collective-permute-done | bytes 524320 | tf_op jit(solution)/shard_map/while/body/eval_jaxpr/ppermute | solution.py:57
  463.1 9.8 %collective-permute-done.3 = bf16[2,2,128,512]{3,2,1,0:T(8,128)(2,1)S(1)} collective-permute-done((bf16[2,2,128,512]{3,2,1,0:T(8,128)(2,1)S(1)}, bf16[2,2,128,512]{3,2,1,0:T(8,128)(2,1)S(1)}, u32[]{:S(2)}, u32[]{:S(2)}) %collective-permute-start.3) | collective-permute-done | bytes 524320 | tf_op jit(solution)/shard_map/while/body/eval_jaxpr/ppermute | solution.py:57
  489.0 5.5 collective-permute-start
  494.8 6.1 %collective-permute-done = bf16[2,2,128,512]{3,2,1,0:T(8,128)(2,1)} collective-permute-done((bf16[2,2,128,512]{3,2,1,0:T(8,128)(2,1)}, bf16[2,2,128,512]{3,2,1,0:T(8,128)(2,1)}, u32[]{:S(2)}, u32[]{:S(2)}) %collective-permute-start) | collective-permute-done | bytes 524320 | tf_op jit(solution)/shard_map/while/body/eval_jaxpr/ppermute | solution.py:22
  503.5 11.9 %collective-permute-done.1 = bf16[2,2,128,512]{3,2,1,0:T(8,128)(2,1)S(1)} collective-permute-done((bf16[2,2,128,512]{3,2,1,0:T(8,128)(2,1)S(1)}, bf16[2,2,128,512]{3,2,1,0:T(8,128)(2,1)S(1)}, u32[]{:S(2)}, u32[]{:S(2)}) %collective-permute-start.1) | collective-permute-done | bytes 524320 | tf_op jit(solution)/shard_map/while/body/eval_jaxpr/ppermute | solution.py:57
  515.5 11.1 %collective-permute-done.2 = bf16[2,2,128,512]{3,2,1,0:T(8,128)(2,1)S(1)} collective-permute-done((bf16[2,2,128,512]{3,2,1,0:T(8,128)(2,1)S(1)}, bf16[2,2,128,512]{3,2,1,0:T(8,128)(2,1)S(1)}, u32[]{:S(2)}, u32[]{:S(2)}) %collective-permute-start.2) | collective-permute-done | bytes 524320 | tf_op jit(solution)/shard_map/while/body/eval_jaxpr/ppermute | solution.py:57
  526.6 9.9 %collective-permute-done.3 = bf16[2,2,128,512]{3,2,1,0:T(8,128)(2,1)S(1)} collective-permute-done((bf16[2,2,128,512]{3,2,1,0:T(8,128)(2,1)S(1)}, bf16[2,2,128,512]{3,2,1,0:T(8,128)(2,1)S(1)}, u32[]{:S(2)}, u32[]{:S(2)}) %collective-permute-start.3) | collective-permute-done | bytes 524320 | tf_op jit(solution)/shard_map/while/body/eval_jaxpr/ppermute | solution.py:57
  551.8 18.8 %collective-permute-start.7 = (bf16[2,1,2,128,512]{4,3,2,1,0:T(8,128)(2,1)S(1)}, bf16[2,1,2,128,512]{4,3,2,1,0:T(8,128)(2,1)S(1)}, u32[]{:S(2)}, u32[]{:S(2)}) collective-permute-start(bf16[2,1,2,128,512]{4,3,2,1,0:T(8,128)(2,1)S(1)} %convert_element_type.69), channel_id=1, source_target_pairs={{0,4},{4,8},{8,12},{12,16},{16,20},{20,24},{24,28},{1,5},{5,9},{9,... | collective-permute-start | bytes 1572872 | tf_op jit(solution)/shard_map/ppermute | solution.py:33
  573.2 3.5 collective-permute-done.7
  576.7 5.0 collective-permute-done.8
  583.0 4.2 collective-permute-start.9
  588.5 5.4 fusion.70
  (333 shorter events, 152.9 us)
Async XLA Ops:
  2.8 30.7 %copy-start.9 = (f32[2,1,2,128,512]{4,3,2,1,0:T(8,128)S(1)}, f32[2,1,2,128,512]{4,3,2,1,0:T(8,128)}, u32[]{:S(2)}) copy-start(f32[2,1,2,128,512]{4,3,2,1,0:T(8,128)} %param.7) | copy-start | bytes 3145732
  3.4 30.0 %copy-start.14 = (bf16[256,512]{1,0:T(8,128)(2,1)}, bf16[256,512]{1,0:T(8,128)(2,1)S(1)}, u32[]{:S(2)}) copy-start(bf16[256,512]{1,0:T(8,128)(2,1)S(1)} %fusion.30) | copy-start | bytes 786436
  3.5 15.8 %collective-permute-start.4 = (bf16[2,2,128,512]{3,2,1,0:T(8,128)(2,1)S(1)}, bf16[2,2,128,512]{3,2,1,0:T(8,128)(2,1)S(1)}, u32[]{:S(2)}, u32[]{:S(2)}) collective-permute-start(bf16[2,2,128,512]{3,2,1,0:T(8,128)(2,1)S(1)} %pad_maximum_fusion.3), channel_id=1, source_target_pairs={{0,1},{1,2},{2,3},{3,0},{4,5},{5,6},{6,7},{7,4},{8,9},{9,10},{10,1... | collective-permute-start | bytes 1572872 | tf_op jit(solution)/shard_map/ppermute | solution.py:57
  19.3 14.1 %collective-permute-start.5 = (bf16[2,2,128,512]{3,2,1,0:T(8,128)(2,1)S(1)}, bf16[2,2,128,512]{3,2,1,0:T(8,128)(2,1)}, u32[]{:S(2)}, u32[]{:S(2)}) collective-permute-start(bf16[2,2,128,512]{3,2,1,0:T(8,128)(2,1)S(1)} %collective-permute-done.4), channel_id=1, source_target_pairs={{0,1},{1,2},{2,3},{3,0},{4,5},{5,6},{6,7},{7,4},{8,9},{9,10},{10,1... | collective-permute-start | bytes 1572872 | tf_op jit(solution)/shard_map/ppermute | solution.py:57
  33.4 13.5 %collective-permute-start.6 = (bf16[2,2,128,512]{3,2,1,0:T(8,128)(2,1)}, bf16[2,2,128,512]{3,2,1,0:T(8,128)(2,1)}, u32[]{:S(2)}, u32[]{:S(2)}) collective-permute-start(bf16[2,2,128,512]{3,2,1,0:T(8,128)(2,1)} %collective-permute-done.5), channel_id=1, source_target_pairs={{0,1},{1,2},{2,3},{3,0},{4,5},{5,6},{6,7},{7,4},{8,9},{9,10},{10,1... | collective-permute-start | bytes 1572872 | tf_op jit(solution)/shard_map/ppermute | solution.py:57
  68.9 12.0 %collective-permute-start = (bf16[2,2,128,512]{3,2,1,0:T(8,128)(2,1)}, bf16[2,2,128,512]{3,2,1,0:T(8,128)(2,1)}, u32[]{:S(2)}, u32[]{:S(2)}) collective-permute-start(bf16[2,2,128,512]{3,2,1,0:T(8,128)(2,1)} %bitcast.201), channel_id=1, source_target_pairs={{0,4},{4,8},{8,12},{12,16},{16,20},{20,24},{24,28},{1,5},{5,9},{9,... | collective-permute-start | bytes 1572872 | tf_op jit(solution)/shard_map/while/body/eval_jaxpr/ppermute | solution.py:22
  83.3 33.5 %copy-start.1 = (bf16[256,512]{1,0:T(8,128)(2,1)}, bf16[256,512]{1,0:T(8,128)(2,1)S(1)}, u32[]{:S(2)}) copy-start(bf16[256,512]{1,0:T(8,128)(2,1)S(1)} %fusion.169) | copy-start | bytes 786436 | tf_op jit(solution)/shard_map/while
  83.4 10.4 %collective-permute-start.1 = (bf16[2,2,128,512]{3,2,1,0:T(8,128)(2,1)S(1)}, bf16[2,2,128,512]{3,2,1,0:T(8,128)(2,1)S(1)}, u32[]{:S(2)}, u32[]{:S(2)}) collective-permute-start(bf16[2,2,128,512]{3,2,1,0:T(8,128)(2,1)S(1)} %pad_maximum_fusion.9), channel_id=1, source_target_pairs={{0,1},{1,2},{2,3},{3,0},{4,5},{5,6},{6,7},{7,4},{8,9},{9,10},{10,1... | collective-permute-start | bytes 1572872 | tf_op jit(solution)/shard_map/while/body/eval_jaxpr/ppermute | solution.py:57
  93.8 10.9 %collective-permute-start.2 = (bf16[2,2,128,512]{3,2,1,0:T(8,128)(2,1)S(1)}, bf16[2,2,128,512]{3,2,1,0:T(8,128)(2,1)S(1)}, u32[]{:S(2)}, u32[]{:S(2)}) collective-permute-start(bf16[2,2,128,512]{3,2,1,0:T(8,128)(2,1)S(1)} %collective-permute-done.1), channel_id=1, source_target_pairs={{0,1},{1,2},{2,3},{3,0},{4,5},{5,6},{6,7},{7,4},{8,9},{9,10},{10,1... | collective-permute-start | bytes 1572872 | tf_op jit(solution)/shard_map/while/body/eval_jaxpr/ppermute | solution.py:57
  104.7 12.1 %collective-permute-start.3 = (bf16[2,2,128,512]{3,2,1,0:T(8,128)(2,1)S(1)}, bf16[2,2,128,512]{3,2,1,0:T(8,128)(2,1)S(1)}, u32[]{:S(2)}, u32[]{:S(2)}) collective-permute-start(bf16[2,2,128,512]{3,2,1,0:T(8,128)(2,1)S(1)} %collective-permute-done.2), channel_id=1, source_target_pairs={{0,1},{1,2},{2,3},{3,0},{4,5},{5,6},{6,7},{7,4},{8,9},{9,10},{10,1... | collective-permute-start | bytes 1572872 | tf_op jit(solution)/shard_map/while/body/eval_jaxpr/ppermute | solution.py:57
  132.8 19.1 %collective-permute-start = (bf16[2,2,128,512]{3,2,1,0:T(8,128)(2,1)}, bf16[2,2,128,512]{3,2,1,0:T(8,128)(2,1)}, u32[]{:S(2)}, u32[]{:S(2)}) collective-permute-start(bf16[2,2,128,512]{3,2,1,0:T(8,128)(2,1)} %bitcast.201), channel_id=1, source_target_pairs={{0,4},{4,8},{8,12},{12,16},{16,20},{20,24},{24,28},{1,5},{5,9},{9,... | collective-permute-start | bytes 1572872 | tf_op jit(solution)/shard_map/while/body/eval_jaxpr/ppermute | solution.py:22
  154.4 35.2 %copy-start.1 = (bf16[256,512]{1,0:T(8,128)(2,1)}, bf16[256,512]{1,0:T(8,128)(2,1)S(1)}, u32[]{:S(2)}) copy-start(bf16[256,512]{1,0:T(8,128)(2,1)S(1)} %fusion.169) | copy-start | bytes 786436 | tf_op jit(solution)/shard_map/while
  154.5 12.1 %collective-permute-start.1 = (bf16[2,2,128,512]{3,2,1,0:T(8,128)(2,1)S(1)}, bf16[2,2,128,512]{3,2,1,0:T(8,128)(2,1)S(1)}, u32[]{:S(2)}, u32[]{:S(2)}) collective-permute-start(bf16[2,2,128,512]{3,2,1,0:T(8,128)(2,1)S(1)} %pad_maximum_fusion.9), channel_id=1, source_target_pairs={{0,1},{1,2},{2,3},{3,0},{4,5},{5,6},{6,7},{7,4},{8,9},{9,10},{10,1... | collective-permute-start | bytes 1572872 | tf_op jit(solution)/shard_map/while/body/eval_jaxpr/ppermute | solution.py:57
  166.6 13.2 %collective-permute-start.2 = (bf16[2,2,128,512]{3,2,1,0:T(8,128)(2,1)S(1)}, bf16[2,2,128,512]{3,2,1,0:T(8,128)(2,1)S(1)}, u32[]{:S(2)}, u32[]{:S(2)}) collective-permute-start(bf16[2,2,128,512]{3,2,1,0:T(8,128)(2,1)S(1)} %collective-permute-done.1), channel_id=1, source_target_pairs={{0,1},{1,2},{2,3},{3,0},{4,5},{5,6},{6,7},{7,4},{8,9},{9,10},{10,1... | collective-permute-start | bytes 1572872 | tf_op jit(solution)/shard_map/while/body/eval_jaxpr/ppermute | solution.py:57
  179.8 9.8 %collective-permute-start.3 = (bf16[2,2,128,512]{3,2,1,0:T(8,128)(2,1)S(1)}, bf16[2,2,128,512]{3,2,1,0:T(8,128)(2,1)S(1)}, u32[]{:S(2)}, u32[]{:S(2)}) collective-permute-start(bf16[2,2,128,512]{3,2,1,0:T(8,128)(2,1)S(1)} %collective-permute-done.2), channel_id=1, source_target_pairs={{0,1},{1,2},{2,3},{3,0},{4,5},{5,6},{6,7},{7,4},{8,9},{9,10},{10,1... | collective-permute-start | bytes 1572872 | tf_op jit(solution)/shard_map/while/body/eval_jaxpr/ppermute | solution.py:57
  205.6 12.1 %collective-permute-start = (bf16[2,2,128,512]{3,2,1,0:T(8,128)(2,1)}, bf16[2,2,128,512]{3,2,1,0:T(8,128)(2,1)}, u32[]{:S(2)}, u32[]{:S(2)}) collective-permute-start(bf16[2,2,128,512]{3,2,1,0:T(8,128)(2,1)} %bitcast.201), channel_id=1, source_target_pairs={{0,4},{4,8},{8,12},{12,16},{16,20},{20,24},{24,28},{1,5},{5,9},{9,... | collective-permute-start | bytes 1572872 | tf_op jit(solution)/shard_map/while/body/eval_jaxpr/ppermute | solution.py:22
  220.2 33.3 %copy-start.1 = (bf16[256,512]{1,0:T(8,128)(2,1)}, bf16[256,512]{1,0:T(8,128)(2,1)S(1)}, u32[]{:S(2)}) copy-start(bf16[256,512]{1,0:T(8,128)(2,1)S(1)} %fusion.169) | copy-start | bytes 786436 | tf_op jit(solution)/shard_map/while
  220.3 12.1 %collective-permute-start.1 = (bf16[2,2,128,512]{3,2,1,0:T(8,128)(2,1)S(1)}, bf16[2,2,128,512]{3,2,1,0:T(8,128)(2,1)S(1)}, u32[]{:S(2)}, u32[]{:S(2)}) collective-permute-start(bf16[2,2,128,512]{3,2,1,0:T(8,128)(2,1)S(1)} %pad_maximum_fusion.9), channel_id=1, source_target_pairs={{0,1},{1,2},{2,3},{3,0},{4,5},{5,6},{6,7},{7,4},{8,9},{9,10},{10,1... | collective-permute-start | bytes 1572872 | tf_op jit(solution)/shard_map/while/body/eval_jaxpr/ppermute | solution.py:57
  232.4 11.2 %collective-permute-start.2 = (bf16[2,2,128,512]{3,2,1,0:T(8,128)(2,1)S(1)}, bf16[2,2,128,512]{3,2,1,0:T(8,128)(2,1)S(1)}, u32[]{:S(2)}, u32[]{:S(2)}) collective-permute-start(bf16[2,2,128,512]{3,2,1,0:T(8,128)(2,1)S(1)} %collective-permute-done.1), channel_id=1, source_target_pairs={{0,1},{1,2},{2,3},{3,0},{4,5},{5,6},{6,7},{7,4},{8,9},{9,10},{10,1... | collective-permute-start | bytes 1572872 | tf_op jit(solution)/shard_map/while/body/eval_jaxpr/ppermute | solution.py:57
  243.6 9.8 %collective-permute-start.3 = (bf16[2,2,128,512]{3,2,1,0:T(8,128)(2,1)S(1)}, bf16[2,2,128,512]{3,2,1,0:T(8,128)(2,1)S(1)}, u32[]{:S(2)}, u32[]{:S(2)}) collective-permute-start(bf16[2,2,128,512]{3,2,1,0:T(8,128)(2,1)S(1)} %collective-permute-done.2), channel_id=1, source_target_pairs={{0,1},{1,2},{2,3},{3,0},{4,5},{5,6},{6,7},{7,4},{8,9},{9,10},{10,1... | collective-permute-start | bytes 1572872 | tf_op jit(solution)/shard_map/while/body/eval_jaxpr/ppermute | solution.py:57
  268.4 24.3 %copy-start.2 = (f32[2,1,2,128,512]{3,4,2,0,1:T(8,128)}, f32[2,1,2,128,512]{3,4,2,0,1:T(8,128)S(1)}, u32[]{:S(2)}) copy-start(f32[2,1,2,128,512]{3,4,2,0,1:T(8,128)S(1)} %get-tuple-element.160) | copy-start | bytes 3145732 | tf_op jit(solution)/shard_map/while
  269.5 22.0 %collective-permute-start = (bf16[2,2,128,512]{3,2,1,0:T(8,128)(2,1)}, bf16[2,2,128,512]{3,2,1,0:T(8,128)(2,1)}, u32[]{:S(2)}, u32[]{:S(2)}) collective-permute-start(bf16[2,2,128,512]{3,2,1,0:T(8,128)(2,1)} %bitcast.201), channel_id=1, source_target_pairs={{0,4},{4,8},{8,12},{12,16},{16,20},{20,24},{24,28},{1,5},{5,9},{9,... | collective-permute-start | bytes 1572872 | tf_op jit(solution)/shard_map/while/body/eval_jaxpr/ppermute | solution.py:22
  294.0 31.0 %copy-start.1 = (bf16[256,512]{1,0:T(8,128)(2,1)}, bf16[256,512]{1,0:T(8,128)(2,1)S(1)}, u32[]{:S(2)}) copy-start(bf16[256,512]{1,0:T(8,128)(2,1)S(1)} %fusion.169) | copy-start | bytes 786436 | tf_op jit(solution)/shard_map/while
  294.0 11.1 %collective-permute-start.1 = (bf16[2,2,128,512]{3,2,1,0:T(8,128)(2,1)S(1)}, bf16[2,2,128,512]{3,2,1,0:T(8,128)(2,1)S(1)}, u32[]{:S(2)}, u32[]{:S(2)}) collective-permute-start(bf16[2,2,128,512]{3,2,1,0:T(8,128)(2,1)S(1)} %pad_maximum_fusion.9), channel_id=1, source_target_pairs={{0,1},{1,2},{2,3},{3,0},{4,5},{5,6},{6,7},{7,4},{8,9},{9,10},{10,1... | collective-permute-start | bytes 1572872 | tf_op jit(solution)/shard_map/while/body/eval_jaxpr/ppermute | solution.py:57
  305.1 10.1 %collective-permute-start.2 = (bf16[2,2,128,512]{3,2,1,0:T(8,128)(2,1)S(1)}, bf16[2,2,128,512]{3,2,1,0:T(8,128)(2,1)S(1)}, u32[]{:S(2)}, u32[]{:S(2)}) collective-permute-start(bf16[2,2,128,512]{3,2,1,0:T(8,128)(2,1)S(1)} %collective-permute-done.1), channel_id=1, source_target_pairs={{0,1},{1,2},{2,3},{3,0},{4,5},{5,6},{6,7},{7,4},{8,9},{9,10},{10,1... | collective-permute-start | bytes 1572872 | tf_op jit(solution)/shard_map/while/body/eval_jaxpr/ppermute | solution.py:57
  315.1 9.8 %collective-permute-start.3 = (bf16[2,2,128,512]{3,2,1,0:T(8,128)(2,1)S(1)}, bf16[2,2,128,512]{3,2,1,0:T(8,128)(2,1)S(1)}, u32[]{:S(2)}, u32[]{:S(2)}) collective-permute-start(bf16[2,2,128,512]{3,2,1,0:T(8,128)(2,1)S(1)} %collective-permute-done.2), channel_id=1, source_target_pairs={{0,1},{1,2},{2,3},{3,0},{4,5},{5,6},{6,7},{7,4},{8,9},{9,10},{10,1... | collective-permute-start | bytes 1572872 | tf_op jit(solution)/shard_map/while/body/eval_jaxpr/ppermute | solution.py:57
  341.0 18.3 %collective-permute-start = (bf16[2,2,128,512]{3,2,1,0:T(8,128)(2,1)}, bf16[2,2,128,512]{3,2,1,0:T(8,128)(2,1)}, u32[]{:S(2)}, u32[]{:S(2)}) collective-permute-start(bf16[2,2,128,512]{3,2,1,0:T(8,128)(2,1)} %bitcast.201), channel_id=1, source_target_pairs={{0,4},{4,8},{8,12},{12,16},{16,20},{20,24},{24,28},{1,5},{5,9},{9,... | collective-permute-start | bytes 1572872 | tf_op jit(solution)/shard_map/while/body/eval_jaxpr/ppermute | solution.py:22
  361.7 36.9 %copy-start.1 = (bf16[256,512]{1,0:T(8,128)(2,1)}, bf16[256,512]{1,0:T(8,128)(2,1)S(1)}, u32[]{:S(2)}) copy-start(bf16[256,512]{1,0:T(8,128)(2,1)S(1)} %fusion.169) | copy-start | bytes 786436 | tf_op jit(solution)/shard_map/while
  361.8 13.0 %collective-permute-start.1 = (bf16[2,2,128,512]{3,2,1,0:T(8,128)(2,1)S(1)}, bf16[2,2,128,512]{3,2,1,0:T(8,128)(2,1)S(1)}, u32[]{:S(2)}, u32[]{:S(2)}) collective-permute-start(bf16[2,2,128,512]{3,2,1,0:T(8,128)(2,1)S(1)} %pad_maximum_fusion.9), channel_id=1, source_target_pairs={{0,1},{1,2},{2,3},{3,0},{4,5},{5,6},{6,7},{7,4},{8,9},{9,10},{10,1... | collective-permute-start | bytes 1572872 | tf_op jit(solution)/shard_map/while/body/eval_jaxpr/ppermute | solution.py:57
  374.8 14.1 %collective-permute-start.2 = (bf16[2,2,128,512]{3,2,1,0:T(8,128)(2,1)S(1)}, bf16[2,2,128,512]{3,2,1,0:T(8,128)(2,1)S(1)}, u32[]{:S(2)}, u32[]{:S(2)}) collective-permute-start(bf16[2,2,128,512]{3,2,1,0:T(8,128)(2,1)S(1)} %collective-permute-done.1), channel_id=1, source_target_pairs={{0,1},{1,2},{2,3},{3,0},{4,5},{5,6},{6,7},{7,4},{8,9},{9,10},{10,1... | collective-permute-start | bytes 1572872 | tf_op jit(solution)/shard_map/while/body/eval_jaxpr/ppermute | solution.py:57
  388.8 9.8 %collective-permute-start.3 = (bf16[2,2,128,512]{3,2,1,0:T(8,128)(2,1)S(1)}, bf16[2,2,128,512]{3,2,1,0:T(8,128)(2,1)S(1)}, u32[]{:S(2)}, u32[]{:S(2)}) collective-permute-start(bf16[2,2,128,512]{3,2,1,0:T(8,128)(2,1)S(1)} %collective-permute-done.2), channel_id=1, source_target_pairs={{0,1},{1,2},{2,3},{3,0},{4,5},{5,6},{6,7},{7,4},{8,9},{9,10},{10,1... | collective-permute-start | bytes 1572872 | tf_op jit(solution)/shard_map/while/body/eval_jaxpr/ppermute | solution.py:57
  414.7 17.6 %collective-permute-start = (bf16[2,2,128,512]{3,2,1,0:T(8,128)(2,1)}, bf16[2,2,128,512]{3,2,1,0:T(8,128)(2,1)}, u32[]{:S(2)}, u32[]{:S(2)}) collective-permute-start(bf16[2,2,128,512]{3,2,1,0:T(8,128)(2,1)} %bitcast.201), channel_id=1, source_target_pairs={{0,4},{4,8},{8,12},{12,16},{16,20},{20,24},{24,28},{1,5},{5,9},{9,... | collective-permute-start | bytes 1572872 | tf_op jit(solution)/shard_map/while/body/eval_jaxpr/ppermute | solution.py:22
  434.8 38.2 %copy-start.1 = (bf16[256,512]{1,0:T(8,128)(2,1)}, bf16[256,512]{1,0:T(8,128)(2,1)S(1)}, u32[]{:S(2)}) copy-start(bf16[256,512]{1,0:T(8,128)(2,1)S(1)} %fusion.169) | copy-start | bytes 786436 | tf_op jit(solution)/shard_map/while
  434.8 13.6 %collective-permute-start.1 = (bf16[2,2,128,512]{3,2,1,0:T(8,128)(2,1)S(1)}, bf16[2,2,128,512]{3,2,1,0:T(8,128)(2,1)S(1)}, u32[]{:S(2)}, u32[]{:S(2)}) collective-permute-start(bf16[2,2,128,512]{3,2,1,0:T(8,128)(2,1)S(1)} %pad_maximum_fusion.9), channel_id=1, source_target_pairs={{0,1},{1,2},{2,3},{3,0},{4,5},{5,6},{6,7},{7,4},{8,9},{9,10},{10,1... | collective-permute-start | bytes 1572872 | tf_op jit(solution)/shard_map/while/body/eval_jaxpr/ppermute | solution.py:57
  448.4 24.5 %copy-start.6 = (bf16[2,2,128,512]{3,2,1,0:T(8,128)(2,1)}, bf16[2,2,128,512]{3,2,1,0:T(8,128)(2,1)S(1)}, u32[]{:S(2)}) copy-start(bf16[2,2,128,512]{3,2,1,0:T(8,128)(2,1)S(1)} %collective-permute-done.1) | copy-start | bytes 1572868 | tf_op jit(solution)/shard_map/while
  448.4 14.7 %collective-permute-start.2 = (bf16[2,2,128,512]{3,2,1,0:T(8,128)(2,1)S(1)}, bf16[2,2,128,512]{3,2,1,0:T(8,128)(2,1)S(1)}, u32[]{:S(2)}, u32[]{:S(2)}) collective-permute-start(bf16[2,2,128,512]{3,2,1,0:T(8,128)(2,1)S(1)} %collective-permute-done.1), channel_id=1, source_target_pairs={{0,1},{1,2},{2,3},{3,0},{4,5},{5,6},{6,7},{7,4},{8,9},{9,10},{10,1... | collective-permute-start | bytes 1572872 | tf_op jit(solution)/shard_map/while/body/eval_jaxpr/ppermute | solution.py:57
  463.1 9.8 %collective-permute-start.3 = (bf16[2,2,128,512]{3,2,1,0:T(8,128)(2,1)S(1)}, bf16[2,2,128,512]{3,2,1,0:T(8,128)(2,1)S(1)}, u32[]{:S(2)}, u32[]{:S(2)}) collective-permute-start(bf16[2,2,128,512]{3,2,1,0:T(8,128)(2,1)S(1)} %collective-permute-done.2), channel_id=1, source_target_pairs={{0,1},{1,2},{2,3},{3,0},{4,5},{5,6},{6,7},{7,4},{8,9},{9,10},{10,1... | collective-permute-start | bytes 1572872 | tf_op jit(solution)/shard_map/while/body/eval_jaxpr/ppermute | solution.py:57
  489.0 11.9 %collective-permute-start = (bf16[2,2,128,512]{3,2,1,0:T(8,128)(2,1)}, bf16[2,2,128,512]{3,2,1,0:T(8,128)(2,1)}, u32[]{:S(2)}, u32[]{:S(2)}) collective-permute-start(bf16[2,2,128,512]{3,2,1,0:T(8,128)(2,1)} %bitcast.201), channel_id=1, source_target_pairs={{0,4},{4,8},{8,12},{12,16},{16,20},{20,24},{24,28},{1,5},{5,9},{9,... | collective-permute-start | bytes 1572872 | tf_op jit(solution)/shard_map/while/body/eval_jaxpr/ppermute | solution.py:22
  503.4 33.2 %copy-start.1 = (bf16[256,512]{1,0:T(8,128)(2,1)}, bf16[256,512]{1,0:T(8,128)(2,1)S(1)}, u32[]{:S(2)}) copy-start(bf16[256,512]{1,0:T(8,128)(2,1)S(1)} %fusion.169) | copy-start | bytes 786436 | tf_op jit(solution)/shard_map/while
  503.4 12.0 %collective-permute-start.1 = (bf16[2,2,128,512]{3,2,1,0:T(8,128)(2,1)S(1)}, bf16[2,2,128,512]{3,2,1,0:T(8,128)(2,1)S(1)}, u32[]{:S(2)}, u32[]{:S(2)}) collective-permute-start(bf16[2,2,128,512]{3,2,1,0:T(8,128)(2,1)S(1)} %pad_maximum_fusion.9), channel_id=1, source_target_pairs={{0,1},{1,2},{2,3},{3,0},{4,5},{5,6},{6,7},{7,4},{8,9},{9,10},{10,1... | collective-permute-start | bytes 1572872 | tf_op jit(solution)/shard_map/while/body/eval_jaxpr/ppermute | solution.py:57
  515.5 11.1 %collective-permute-start.2 = (bf16[2,2,128,512]{3,2,1,0:T(8,128)(2,1)S(1)}, bf16[2,2,128,512]{3,2,1,0:T(8,128)(2,1)S(1)}, u32[]{:S(2)}, u32[]{:S(2)}) collective-permute-start(bf16[2,2,128,512]{3,2,1,0:T(8,128)(2,1)S(1)} %collective-permute-done.1), channel_id=1, source_target_pairs={{0,1},{1,2},{2,3},{3,0},{4,5},{5,6},{6,7},{7,4},{8,9},{9,10},{10,1... | collective-permute-start | bytes 1572872 | tf_op jit(solution)/shard_map/while/body/eval_jaxpr/ppermute | solution.py:57
  526.6 10.0 %collective-permute-start.3 = (bf16[2,2,128,512]{3,2,1,0:T(8,128)(2,1)S(1)}, bf16[2,2,128,512]{3,2,1,0:T(8,128)(2,1)S(1)}, u32[]{:S(2)}, u32[]{:S(2)}) collective-permute-start(bf16[2,2,128,512]{3,2,1,0:T(8,128)(2,1)S(1)} %collective-permute-done.2), channel_id=1, source_target_pairs={{0,1},{1,2},{2,3},{3,0},{4,5},{5,6},{6,7},{7,4},{8,9},{9,10},{10,1... | collective-permute-start | bytes 1572872 | tf_op jit(solution)/shard_map/while/body/eval_jaxpr/ppermute | solution.py:57
  551.7 42.2 %copy-start.11 = (f32[2,1,2,128,512]{4,3,2,1,0:T(8,128)}, f32[2,1,2,128,512]{4,3,2,1,0:T(8,128)S(1)}, u32[]{:S(2)}) copy-start(f32[2,1,2,128,512]{4,3,2,1,0:T(8,128)S(1)} %copy.26) | copy-start | bytes 3145732
  551.7 35.4 %copy-start.15 = (f32[1,128,512]{2,1,0:T(8,128)S(1)}, f32[1,128,512]{2,1,0:T(8,128)}, u32[]{:S(2)}) copy-start(f32[1,128,512]{2,1,0:T(8,128)} %param.8) | copy-start | bytes 786436
  551.8 24.9 %collective-permute-start.7 = (bf16[2,1,2,128,512]{4,3,2,1,0:T(8,128)(2,1)S(1)}, bf16[2,1,2,128,512]{4,3,2,1,0:T(8,128)(2,1)S(1)}, u32[]{:S(2)}, u32[]{:S(2)}) collective-permute-start(bf16[2,1,2,128,512]{4,3,2,1,0:T(8,128)(2,1)S(1)} %convert_element_type.69), channel_id=1, source_target_pairs={{0,4},{4,8},{8,12},{12,16},{16,20},{20,24},{24,28},{1,5},{5,9},{9,... | collective-permute-start | bytes 1572872 | tf_op jit(solution)/shard_map/ppermute | solution.py:33
  570.6 11.1 %collective-permute-start.8 = (bf16[2,1,2,128,512]{4,3,2,1,0:T(8,128)(2,1)S(1)}, bf16[2,1,2,128,512]{4,3,2,1,0:T(8,128)(2,1)S(1)}, u32[]{:S(2)}, u32[]{:S(2)}) collective-permute-start(bf16[2,1,2,128,512]{4,3,2,1,0:T(8,128)(2,1)S(1)} %convert_element_type.69), channel_id=1, source_target_pairs={{4,0},{8,4},{12,8},{16,12},{20,16},{24,20},{28,24},{5,1},{9,5},{13... | collective-permute-start | bytes 1572872 | tf_op jit(solution)/shard_map/ppermute | solution.py:35
  581.7 5.5 collective-permute-start.10
  583.0 4.9 collective-permute-start.9
  (46 other events, 374.5 us)
